TPU v7x, 512 devices: a whole 4x4x16 slice. The times are simulated.
512 devices in a mesh: req: 64 (over z, y), hid: 8 (over x, core).
Axes of the slice: x: 4, y: 4, z: 16, core: 2. Of those that a mesh axis runs over, the one named last changes fastest.
Arguments:
- resid: bfloat16 [8192, 1024], P('req'), may hold values from -6 to 6
- attn_gain: float32 [1024], replicated, may hold values from 0.25 to 1.75
- w_query: bfloat16 [1024, 1024], P(None, 'hid'), may hold values from -4 to 4
- w_key: bfloat16 [1024, 1024], P(None, 'hid'), may hold values from -1 to 1
- w_value: bfloat16 [1024, 1024], P(None, 'hid'), may hold values from -0.1875 to 0.1875
- w_attn_out: bfloat16 [1024, 1024], P('hid'), may hold values from -0.1875 to 0.1875
- cache: bfloat16 [2048, 2, 16, 1024], P('req', None, None, 'hid'), may hold values from -48 to 48
- cache_lens: int32 [2048], P('req'), may hold values from 1 to 16
- seg_ids: int32 [64, 96], P('req'), may hold values from 0 to 3, never falling along the last dimension, each value on 1 to 48 neighbouring positions
- ffn_gain: float32 [1024], replicated, may hold values from 0.25 to 1.75
- router: bfloat16 [1024, 16], replicated, may hold values from -0.078125 to 0.078125
- routes: int32 [8192, 2], P('req'), may hold values from 0 to 15, all different within a row; in each aligned block of 16 rows (0 to 15, 16 to 31, ...) at most 3 rows name the same one
- w_in: bfloat16 [2, 1024, 45056], P(None, None, ('req', 'hid')), may hold values from -0.1875 to 0.1875
- w_out: bfloat16 [45056, 1024], P('req'), may hold values from -0.109375 to 0.109375
Outputs:
- layer_out: bfloat16 [8192, 1024], P(('req', 'hid'))
Inputs may be any that keep to these rules, and one draw needn't show every extreme that they name: `routes`: in every aligned block of 16 rows no expert is named more than 3 times, so no assignment is dropped.
All inputs are finite; a program needn't handle non-finite values.
Results may differ from a plain program's by a relative error of at most 0.012.
The roundings to bfloat16 on the way count: a program that leaves them out, or rounds other values in their place, can miss the bound.
Values may be sent and summed in bfloat16 or wider, within the bound.
No kernel may reach another device: no remote copies, remote signals or barrier semaphores. Data moves between devices by JAX's collectives and lax.ppermute only.
A program may use at most 64 MiB of HBM per device.

v0:
```python
import jax
import jax.numpy as jnp
from jax import lax
from jax.sharding import PartitionSpec as P

HDIM = 64
EPS = 1e-06


def rms_scale(values, gain):
    values = values.astype(jnp.float32)
    inverse = lax.rsqrt(jnp.mean(values * values, axis=-1, keepdims=True) + EPS)
    return (values * inverse * gain).astype(jnp.bfloat16)


def softmax_bf16(scores, allowed):
    scores = jnp.where(allowed, scores, -jnp.inf)
    highest = jnp.max(scores, axis=-1, keepdims=True)
    weights = jnp.exp(scores - highest)
    return (weights / jnp.sum(weights, axis=-1, keepdims=True)).astype(jnp.bfloat16)


def attend(normed, w_query, w_key, w_value, segments, cached, lengths):
    heads = w_query.shape[1] // HDIM
    scale = HDIM ** (-0.5)
    total = normed.shape[0]
    packed = segments.shape[0]
    decoded = total - packed
    slots = cached.shape[2]
    query = (
        jnp.dot(normed, w_query, preferred_element_type=jnp.float32)
        .astype(jnp.bfloat16)
        .reshape(total, heads, HDIM)
    )
    keys = (
        jnp.dot(normed, w_key, preferred_element_type=jnp.float32)
        .astype(jnp.bfloat16)
        .reshape(total, heads, HDIM)
    )
    values = (
        jnp.dot(normed, w_value, preferred_element_type=jnp.float32)
        .astype(jnp.bfloat16)
        .reshape(total, heads, HDIM)
    )
    positions = jnp.arange(packed)
    allowed = (positions[None, :] <= positions[:, None]) & (segments[None, :] == segments[:, None])
    scores = (
        jnp.einsum(
            "qhd,khd->hqk", query[:packed], keys[:packed], preferred_element_type=jnp.float32
        )
        * scale
    )
    weights = softmax_bf16(scores, allowed[None])
    prompt_ctx = jnp.einsum(
        "hqk,khd->qhd", weights, values[:packed], preferred_element_type=jnp.float32
    )
    stored = cached.reshape(decoded, 2, slots, heads, HDIM)
    cached_scores = (
        jnp.einsum(
            "uhd,uchd->uhc", query[packed:], stored[:, 0], preferred_element_type=jnp.float32
        )
        * scale
    )
    own_scores = (
        jnp.sum(
            query[packed:].astype(jnp.float32) * keys[packed:].astype(jnp.float32),
            axis=-1,
            keepdims=True,
        )
        * scale
    )
    valid = jnp.arange(slots)[None, None, :] < lengths[:, None, None]
    allowed_all = jnp.concatenate(
        [jnp.broadcast_to(valid, cached_scores.shape), jnp.ones(own_scores.shape, dtype=bool)],
        axis=-1,
    )
    joined = jnp.concatenate([cached_scores, own_scores], axis=-1)
    weights_dec = softmax_bf16(joined, allowed_all)
    decode_ctx = jnp.einsum(
        "uhc,uchd->uhd", weights_dec[..., :slots], stored[:, 1], preferred_element_type=jnp.float32
    )
    decode_ctx = decode_ctx + weights_dec[..., slots:].astype(jnp.float32) * values[packed:].astype(
        jnp.float32
    )
    context = jnp.concatenate([prompt_ctx, decode_ctx], axis=0)
    return context.reshape(total, heads * HDIM).astype(jnp.bfloat16)


def route_block(chosen, gate_logits, capacity):
    count = chosen.shape[0]
    experts = gate_logits.shape[1]
    flat = chosen.reshape(count * 2)
    onehot = (flat[:, None] == jnp.arange(experts, dtype=jnp.int32)[None, :]).astype(jnp.int32)
    earlier = jnp.cumsum(onehot, axis=0) - onehot
    slot = jnp.sum(earlier * onehot, axis=1)
    target = flat * capacity + slot
    placed = (target[:, None] == jnp.arange(experts * capacity, dtype=jnp.int32)[None, :]).astype(
        jnp.float32
    )
    placed = placed.reshape(count, 2, experts * capacity)
    picked_logits = jnp.sum(
        onehot.reshape(count, 2, experts).astype(jnp.float32) * gate_logits[:, None, :], axis=-1
    )
    gates = jax.nn.sigmoid(picked_logits)
    dispatch = jnp.sum(placed, axis=1).astype(jnp.bfloat16)
    combine_w = jnp.sum(placed * gates[:, :, None], axis=1)
    return (dispatch, combine_w)


def hidden_units(tokens_in, w_in):
    gate_val = jnp.dot(tokens_in, w_in[0], preferred_element_type=jnp.float32)
    up_val = jnp.dot(tokens_in, w_in[1], preferred_element_type=jnp.float32)
    return (jax.nn.gelu(gate_val, approximate=True) * up_val).astype(jnp.bfloat16)


def body(
    resid,
    attn_gain,
    w_query,
    w_key,
    w_value,
    w_attn_out,
    cache,
    cache_lens,
    seg_ids,
    ffn_gain,
    router,
    routes,
    w_in,
    w_out,
):
    req_count = lax.axis_size("req")
    hid_count = lax.axis_size("hid")
    hid_index = lax.axis_index("hid")
    experts = router.shape[1]
    replicas = req_count // experts
    group_rows = resid.shape[0]
    block_rows = group_rows // hid_count
    capacity = max(2, (5 * block_rows + 31) // 32)
    width = resid.shape[1]
    row_start = hid_index * block_rows
    normed = rms_scale(resid, attn_gain)
    context = attend(normed, w_query, w_key, w_value, seg_ids[0], cache, cache_lens)
    partial_mix = jnp.dot(context, w_attn_out, preferred_element_type=jnp.float32)
    mixed = lax.psum(partial_mix, "hid")
    after = resid.astype(jnp.float32) + mixed
    full_ffn = rms_scale(after, ffn_gain)
    own_after = lax.dynamic_slice_in_dim(after, row_start, block_rows, 0)
    logits = jnp.dot(full_ffn, router, preferred_element_type=jnp.float32)
    all_routes = routes.reshape(hid_count, block_rows, 2)
    all_logits = logits.reshape(hid_count, block_rows, experts)
    dispatch_all, combine_all = jax.vmap(
        lambda chosen, gate_logits: route_block(chosen, gate_logits, capacity)
    )(all_routes, all_logits)
    combine_w = lax.dynamic_index_in_dim(combine_all, hid_index, 0, keepdims=False)
    all_tokens = full_ffn.reshape(hid_count, block_rows, width)
    outgoing = jnp.einsum(
        "nbs,nbd->nsd", dispatch_all, all_tokens, preferred_element_type=jnp.float32
    ).astype(jnp.bfloat16)
    outgoing = jnp.broadcast_to(
        outgoing.reshape(hid_count, experts, 1, capacity, width),
        (hid_count, experts, replicas, capacity, width),
    )
    outgoing = outgoing.reshape(hid_count, req_count, capacity, width)
    received = lax.all_to_all(outgoing, "req", split_axis=1, concat_axis=1, tiled=True)
    hidden = hidden_units(received.reshape(hid_count * req_count * capacity, width), w_in)
    stacked = hidden.reshape(hid_count, req_count * capacity, hidden.shape[1])
    projected = jnp.dot(
        lax.all_to_all(stacked, "hid", split_axis=0, concat_axis=2, tiled=True)[0],
        w_out,
        preferred_element_type=jnp.float32,
    ).astype(jnp.bfloat16)[None]
    returned = lax.all_to_all(
        projected.reshape(req_count * capacity, width),
        "req",
        split_axis=0,
        concat_axis=0,
        tiled=True,
    )
    summed = jnp.sum(
        returned.astype(jnp.float32).reshape(experts, replicas, capacity, width), axis=1
    )
    ffn_total = jnp.dot(
        combine_w,
        summed.reshape(experts * capacity, width),
        precision=lax.Precision.HIGHEST,
        preferred_element_type=jnp.float32,
    )
    return (own_after + ffn_total).astype(jnp.bfloat16)


def solution(mesh):
    in_specs = (
        P("req", None),
        P(),
        P(None, "hid"),
        P(None, "hid"),
        P(None, "hid"),
        P("hid", None),
        P("req", None, None, "hid"),
        P("req"),
        P("req", None),
        P(),
        P(),
        P("req", None),
        P(None, None, ("req", "hid")),
        P("req", None),
    )
    out_specs = P(("req", "hid"), None)
    return jax.shard_map(body, mesh=mesh, in_specs=in_specs, out_specs=out_specs, check_vma=False)
```

profile of v0, /device:TPU:8, one launch (start us, length us, event | category | flops | bytes accessed | tf_op | source)
XLA Modules:
  0.0 338.4 jit_solution(14188825207988231362)
XLA Ops:
  6.6 1.2 fusion.15
  7.8 1.3 convolution_convert_fusion.4
  9.4 1.3 convolution_convert_fusion.3
  11.0 1.2 reshape.174
  14.4 0.7 multiply_reduce_fusion
  15.7 1.1 fusion.46
  17.1 0.7 fusion.45
  18.0 79.3 %all-reduce.3.cloned.1.call-done = f32[128,1024]{1,0:T(8,128)} async-done(((f32[128,1024]{1,0:T(8,128)}), f32[128,1024]{1,0:T(8,128)}) %all-reduce.3.cloned.1.call-update) | async-done | bytes 524304 | tf_op jit(solution)/shard_map/psum | solution.py:145
  97.3 1.2 multiply_reduce_fusion.1
  99.3 0.4 convolution_convert_fusion
  99.7 0.4 copy.96
  100.1 0.4 broadcast_in_dim.27
  100.5 158.6 %all_to_all.29 = bf16[8,64,3,1024]{3,0,2,1:T(8,128)(2,1)S(1)} all-to-all(bf16[8,64,3,1024]{3,0,2,1:T(8,128)(2,1)S(1)} %bitcast.73), channel_id=1, replica_groups=mesh['req'=64,'hid'=8] {'req'}, dimensions={1} | all-to-all | bytes 6291456 | tf_op jit(solution)/shard_map/all_to_all | solution.py:165
  259.1 4.6 %copy.97 = bf16[8,64,3,1024]{3,2,1,0:T(4,128)(2,1)} copy(bf16[8,64,3,1024]{3,0,2,1:T(8,128)(2,1)S(1)} %all_to_all.29) | data formatting | bytes 6291456 | tf_op jit(solution)/shard_map/all_to_all | solution.py:165
  263.7 8.9 %reshape.177 = bf16[1536,1024]{1,0:T(8,128)(2,1)} reshape(bf16[8,64,3,1024]{3,2,1,0:T(4,128)(2,1)} %copy.97) | data formatting | bytes 6291456 | tf_op jit(solution)/shard_map/reshape | solution.py:166
  272.6 3.1 fusion.21
  275.7 1.1 fusion.1
  276.8 0.3 reshape.178
  277.2 13.2 %all_to_all.30 = bf16[8,192,88]{1,2,0:T(8,128)(2,1)S(1)} all-to-all(bf16[8,192,88]{1,2,0:T(8,128)(2,1)S(1)} %copy.98), channel_id=1, replica_groups=mesh['req'=64,'hid'=8] {'hid'}, dimensions={0} | all-to-all | bytes 540672 | tf_op jit(solution)/shard_map/all_to_all | solution.py:169
  290.3 0.5 convolution_convert_fusion.1
  290.9 1.0 all_to_all.24
  291.9 5.9 %all-to-all-start.2 = ((bf16[64,3,1024]{2,1,0:T(4,128)(2,1)}), bf16[64,3,1024]{2,1,0:T(4,128)(2,1)S(1)}, u32[]{:S(2)}, u32[]{:S(2)}) async-start(bf16[64,3,1024]{2,1,0:T(4,128)(2,1)} %all_to_all.24), calls=%async_computation.2 | async-start | bytes 1048576 | tf_op jit(solution)/shard_map/all_to_all | solution.py:173
  297.8 32.6 %all-to-all-done.2 = bf16[64,3,1024]{2,1,0:T(4,128)(2,1)S(1)} async-done(((bf16[64,3,1024]{2,1,0:T(4,128)(2,1)}), bf16[64,3,1024]{2,1,0:T(4,128)(2,1)S(1)}, u32[]{:S(2)}, u32[]{:S(2)}) %all-to-all-start.2) | async-done | bytes 393248 | tf_op jit(solution)/shard_map/all_to_all | solution.py:173
  330.8 0.8 fusion.6
  (81 shorter events, 4.6 us)
Async XLA Ops:
  6.5 283.8 %copy-start = (bf16[704,1024]{1,0:T(8,128)(2,1)S(1)}, bf16[704,1024]{1,0:T(8,128)(2,1)}, u32[]{:S(2)}) copy-start(bf16[704,1024]{1,0:T(8,128)(2,1)} %param.27) | copy-start | bytes 4325380
  6.5 7.3 %copy-start.2 = (bf16[128,1024]{1,0:T(8,128)(2,1)S(1)}, bf16[128,1024]{1,0:T(8,128)(2,1)}, u32[]{:S(2)}) copy-start(bf16[128,1024]{1,0:T(8,128)(2,1)} %param.14) | copy-start | bytes 786436
  6.5 7.3 %copy-start.11 = (f32[1024]{0:T(1024)S(1)}, f32[1024]{0:T(1024)}, u32[]{:S(2)}) copy-start(f32[1024]{0:T(1024)} %param.15) | copy-start | bytes 12292
  6.5 6.2 %copy-start.9 = (s32[32]{0:T(128)S(1)}, s32[32]{0:T(128)}, u32[]{:S(2)}) copy-start(s32[32]{0:T(128)} %param.21) | copy-start | bytes 388
  6.5 6.7 %copy-start.8 = (s32[1,96]{1,0:T(1,128)S(1)}, s32[1,96]{1,0:T(1,128)}, u32[]{:S(2)}) copy-start(s32[1,96]{1,0:T(1,128)} %param.22) | copy-start | bytes 1156
  6.5 7.3 %copy-start.10 = (bf16[1024,128]{1,0:T(8,128)(2,1)S(1)}, bf16[1024,128]{1,0:T(8,128)(2,1)}, u32[]{:S(2)}) copy-start(bf16[1024,128]{1,0:T(8,128)(2,1)} %param.18) | copy-start | bytes 786436
  6.6 90.8 %all-reduce.3.cloned.1.call-start = ((), (), s32[]{:S(2)}) async-start(), calls=%async_computation.3 | async-start | bytes 1048576 | tf_op jit(solution)/shard_map/psum | solution.py:145
  9.2 6.5 %copy-start.3 = (bf16[128,1024]{1,0:T(8,128)(2,1)S(1)}, bf16[128,1024]{1,0:T(8,128)(2,1)}, u32[]{:S(2)}) copy-start(bf16[128,1024]{1,0:T(8,128)(2,1)} %param.19) | copy-start | bytes 786436
  11.0 5.8 %copy-start.7 = (s32[128,2]{0,1:T(2,128)S(1)}, s32[128,2]{0,1:T(2,128)}, u32[]{:S(2)}) copy-start(s32[128,2]{0,1:T(2,128)} %param.25) | copy-start | bytes 3076
  12.8 85.8 %copy-start.6 = (f32[1024]{0:T(1024)S(1)}, f32[1024]{0:T(1024)}, u32[]{:S(2)}) copy-start(f32[1024]{0:T(1024)} %param.23) | copy-start | bytes 12292
  13.8 84.8 %copy-start.5 = (bf16[1024,16]{0,1:T(8,128)(2,1)S(1)}, bf16[1024,16]{0,1:T(8,128)(2,1)}, u32[]{:S(2)}) copy-start(bf16[1024,16]{0,1:T(8,128)(2,1)} %param.24) | copy-start | bytes 98308
  263.7 8.9 %copy-start.4 = (bf16[2,1024,88]{1,2,0:T(8,128)(2,1)S(1)}, bf16[2,1024,88]{1,2,0:T(8,128)(2,1)}, u32[]{:S(2)}) copy-start(bf16[2,1024,88]{1,2,0:T(8,128)(2,1)} %param.26) | copy-start | bytes 1081348
  272.6 3.1 copy-start.1
  291.9 38.5 %all-to-all-start.2 = ((bf16[64,3,1024]{2,1,0:T(4,128)(2,1)}), bf16[64,3,1024]{2,1,0:T(4,128)(2,1)S(1)}, u32[]{:S(2)}, u32[]{:S(2)}) async-start(bf16[64,3,1024]{2,1,0:T(4,128)(2,1)} %all_to_all.24), calls=%async_computation.2 | async-start | bytes 1048576 | tf_op jit(solution)/shard_map/all_to_all | solution.py:173
Sparse Core Ops, SparseCore 0:
  16.9 80.3 all-reduce.2
where the time goes:
time: 339 us; the launch traced here: 338 us
  blocking collectives  172 us (51%)
  waiting for transfers between devices  112 us (33%)
  local copies, waits for them, and re-layouts  18.9 us (6%)
  between operations  13.9 us (4%)
  matrix products  11.1 us (3%)
  starting transfers between devices  5.98 us (2%)
  other arithmetic  5.03 us (1%)
    all_to_all x1, blocking collectives, body(): lax.all_to_all(outgoing, 'req', split_axis=1, concat_axis=1, tiled=True)  159 us
    psum x1, waiting for transfers between devices, body(): mixed = lax.psum(partial_mix, 'hid')  79.3 us
    all_to_all x1, waiting for transfers between devices, body(): lax.all_to_all(projected.reshape(req_count * capacity, width), 'req', spl...  32.6 us
    all_to_all x1, blocking collectives, body(): lax.all_to_all(stacked, 'hid', split_axis=0, concat_axis=2, tiled=True)[0]  13.2 us
    reshape x1, local copies, waits for them, and re-layouts, body(): received.reshape(hid_count * req_count * capacity, width)  8.86 us
  transfers between devices with their start and end apart: 2, of which 2 were waited for; matrix products, arithmetic and copies ran while one was open for 0% of the time, Pallas kernels for 0%

commit v1 on v0

--- a/solution.py
+++ b/solution.py
@@ -142,7 +142,7 @@
     normed = rms_scale(resid, attn_gain)
     context = attend(normed, w_query, w_key, w_value, seg_ids[0], cache, cache_lens)
     partial_mix = jnp.dot(context, w_attn_out, preferred_element_type=jnp.float32)
-    mixed = lax.psum(partial_mix, "hid")
+    mixed = jnp.sum(lax.all_gather(partial_mix, "hid"), axis=0)
     after = resid.astype(jnp.float32) + mixed
     full_ffn = rms_scale(after, ffn_gain)
     own_after = lax.dynamic_slice_in_dim(after, row_start, block_rows, 0)

time: 339 us -> 305 us (0.90)
  waiting for transfers between devices: 112 us -> 75.6 us
    psum x1 -> x0, waiting for transfers between devices: 79.3 us -> none  [body(): mixed = lax.psum(partial_mix, 'hid')]
    all_gather x0 -> x1, waiting for transfers between devices: none -> 43.1 us  [body(): mixed = jnp.sum(lax.all_gather(partial_mix, 'hid'), axis=0)]
where the time goes in v1:
time: 305 us; the launch traced here: 304 us
  blocking collectives  172 us (56%)
  waiting for transfers between devices  75.6 us (25%)
  local copies, waits for them, and re-layouts  18.9 us (6%)
  between operations  13.9 us (5%)
  matrix products  11.1 us (4%)
  other arithmetic  6.6 us (2%)
  starting transfers between devices  5.99 us (2%)
    all_to_all x1, blocking collectives, body(): lax.all_to_all(outgoing, 'req', split_axis=1, concat_axis=1, tiled=True)  161 us
    all_gather x1, waiting for transfers between devices, body(): mixed = jnp.sum(lax.all_gather(partial_mix, 'hid'), axis=0)  43.1 us
    all_to_all x1, waiting for transfers between devices, body(): lax.all_to_all(projected.reshape(req_count * capacity, width), 'req', spl...  32.5 us
    all_to_all x1, blocking collectives, body(): lax.all_to_all(stacked, 'hid', split_axis=0, concat_axis=2, tiled=True)[0]  11.3 us
    reshape x1, local copies, waits for them, and re-layouts, body(): received.reshape(hid_count * req_count * capacity, width)  8.86 us
  transfers between devices with their start and end apart: 2, of which 2 were waited for; matrix products, arithmetic and copies ran while one was open for 0% of the time, Pallas kernels for 0%

profile of v1, /device:TPU:8, one launch (start us, length us, event | category | flops | bytes accessed | tf_op | source)
XLA Modules:
  0.0 304.4 jit_solution(10762042407331182361)
XLA Ops:
  6.6 1.2 fusion.15
  7.8 1.3 convolution_convert_fusion.4
  9.4 1.3 convolution_convert_fusion.3
  11.0 1.2 reshape.174
  14.3 0.7 multiply_reduce_fusion
  15.7 1.0 fusion.46
  17.1 0.7 fusion.45
  18.0 43.1 %all-gather.3.cloned.1.call-done = f32[1024,1024]{1,0:T(8,128)} async-done(((f32[128,1024]{1,0:T(8,128)}), f32[1024,1024]{1,0:T(8,128)}) %all-gather.3.cloned.1.call-update) | async-done | bytes 4194320 | tf_op jit(solution)/shard_map/all_gather | solution.py:145
  61.0 2.6 reduce_sum.105
  64.6 0.4 convolution_convert_fusion
  65.0 0.4 copy.96
  65.4 0.4 broadcast_in_dim.27
  65.8 161.0 %all_to_all.29 = bf16[8,64,3,1024]{3,0,2,1:T(8,128)(2,1)S(1)} all-to-all(bf16[8,64,3,1024]{3,0,2,1:T(8,128)(2,1)S(1)} %bitcast.74), channel_id=1, replica_groups=mesh['req'=64,'hid'=8] {'req'}, dimensions={1} | all-to-all | bytes 6291456 | tf_op jit(solution)/shard_map/all_to_all | solution.py:165
  226.8 4.6 %copy.97 = bf16[8,64,3,1024]{3,2,1,0:T(4,128)(2,1)} copy(bf16[8,64,3,1024]{3,0,2,1:T(8,128)(2,1)S(1)} %all_to_all.29) | data formatting | bytes 6291456 | tf_op jit(solution)/shard_map/all_to_all | solution.py:165
  231.4 8.9 %reshape.177 = bf16[1536,1024]{1,0:T(8,128)(2,1)} reshape(bf16[8,64,3,1024]{3,2,1,0:T(4,128)(2,1)} %copy.97) | data formatting | bytes 6291456 | tf_op jit(solution)/shard_map/reshape | solution.py:166
  240.3 3.1 %fusion.21 = f32[1536,88]{0,1:T(8,128)S(1)} fusion(bf16[1536,1024]{1,0:T(8,128)(2,1)} %reshape.177, bf16[2,1024,88]{1,2,0:T(8,128)(2,1)S(1)} %copy-done.4), kind=kOutput, calls=%fused_computation.41 | convolution fusion | flops 276824064 | bytes 3866624 | tf_op jit(solution)/shard_map/dot_general | solution.py:111
  243.4 1.1 fusion.1
  244.5 0.3 reshape.178
  244.9 11.3 %all_to_all.30 = bf16[8,192,88]{1,2,0:T(8,128)(2,1)S(1)} all-to-all(bf16[8,192,88]{1,2,0:T(8,128)(2,1)S(1)} %copy.98), channel_id=1, replica_groups=mesh['req'=64,'hid'=8] {'hid'}, dimensions={0} | all-to-all | bytes 540672 | tf_op jit(solution)/shard_map/all_to_all | solution.py:169
  256.3 0.5 convolution_convert_fusion.1
  256.8 1.0 all_to_all.24
  257.8 6.0 %all-to-all-start.2 = ((bf16[64,3,1024]{2,1,0:T(4,128)(2,1)}), bf16[64,3,1024]{2,1,0:T(4,128)(2,1)S(1)}, u32[]{:S(2)}, u32[]{:S(2)}) async-start(bf16[64,3,1024]{2,1,0:T(4,128)(2,1)} %all_to_all.24), calls=%async_computation.2 | async-start | bytes 1048576 | tf_op jit(solution)/shard_map/all_to_all | solution.py:173
  263.8 32.5 %all-to-all-done.2 = bf16[64,3,1024]{2,1,0:T(4,128)(2,1)S(1)} async-done(((bf16[64,3,1024]{2,1,0:T(4,128)(2,1)}), bf16[64,3,1024]{2,1,0:T(4,128)(2,1)S(1)}, u32[]{:S(2)}, u32[]{:S(2)}) %all-to-all-start.2) | async-done | bytes 393248 | tf_op jit(solution)/shard_map/all_to_all | solution.py:173
  296.7 0.8 fusion.6
  (82 shorter events, 4.8 us)
Async XLA Ops:
  6.5 249.7 %copy-start = (bf16[704,1024]{1,0:T(8,128)(2,1)S(1)}, bf16[704,1024]{1,0:T(8,128)(2,1)}, u32[]{:S(2)}) copy-start(bf16[704,1024]{1,0:T(8,128)(2,1)} %param.27) | copy-start | bytes 4325380
  6.5 7.3 %copy-start.2 = (bf16[128,1024]{1,0:T(8,128)(2,1)S(1)}, bf16[128,1024]{1,0:T(8,128)(2,1)}, u32[]{:S(2)}) copy-start(bf16[128,1024]{1,0:T(8,128)(2,1)} %param.14) | copy-start | bytes 786436
  6.5 7.3 %copy-start.11 = (f32[1024]{0:T(1024)S(1)}, f32[1024]{0:T(1024)}, u32[]{:S(2)}) copy-start(f32[1024]{0:T(1024)} %param.15) | copy-start | bytes 12292
  6.5 6.2 %copy-start.9 = (s32[32]{0:T(128)S(1)}, s32[32]{0:T(128)}, u32[]{:S(2)}) copy-start(s32[32]{0:T(128)} %param.21) | copy-start | bytes 388
  6.5 6.7 %copy-start.8 = (s32[1,96]{1,0:T(1,128)S(1)}, s32[1,96]{1,0:T(1,128)}, u32[]{:S(2)}) copy-start(s32[1,96]{1,0:T(1,128)} %param.22) | copy-start | bytes 1156
  6.5 7.3 %copy-start.10 = (bf16[1024,128]{1,0:T(8,128)(2,1)S(1)}, bf16[1024,128]{1,0:T(8,128)(2,1)}, u32[]{:S(2)}) copy-start(bf16[1024,128]{1,0:T(8,128)(2,1)} %param.18) | copy-start | bytes 786436
  6.6 54.5 %all-gather.3.cloned.1.call-start = ((), (), s32[]{:S(2)}) async-start(), calls=%async_computation.3 | async-start | bytes 4718592 | tf_op jit(solution)/shard_map/all_gather | solution.py:145
  9.2 6.5 %copy-start.3 = (bf16[128,1024]{1,0:T(8,128)(2,1)S(1)}, bf16[128,1024]{1,0:T(8,128)(2,1)}, u32[]{:S(2)}) copy-start(bf16[128,1024]{1,0:T(8,128)(2,1)} %param.19) | copy-start | bytes 786436
  11.0 5.7 %copy-start.7 = (s32[128,2]{0,1:T(2,128)S(1)}, s32[128,2]{0,1:T(2,128)}, u32[]{:S(2)}) copy-start(s32[128,2]{0,1:T(2,128)} %param.25) | copy-start | bytes 3076
  16.9 46.9 %copy-start.6 = (f32[1024]{0:T(1024)S(1)}, f32[1024]{0:T(1024)}, u32[]{:S(2)}) copy-start(f32[1024]{0:T(1024)} %param.23) | copy-start | bytes 12292
  61.0 2.9 copy-start.5
  231.4 8.9 %copy-start.4 = (bf16[2,1024,88]{1,2,0:T(8,128)(2,1)S(1)}, bf16[2,1024,88]{1,2,0:T(8,128)(2,1)}, u32[]{:S(2)}) copy-start(bf16[2,1024,88]{1,2,0:T(8,128)(2,1)} %param.26) | copy-start | bytes 1081348
  240.3 3.1 %copy-start.1 = (bf16[1536,1024]{1,0:T(8,128)(2,1)S(1)}, bf16[1536,1024]{1,0:T(8,128)(2,1)}, u32[]{:S(2)}) copy-start(bf16[1536,1024]{1,0:T(8,128)(2,1)} %reshape.177) | copy-start | bytes 9437188
  257.8 38.5 %all-to-all-start.2 = ((bf16[64,3,1024]{2,1,0:T(4,128)(2,1)}), bf16[64,3,1024]{2,1,0:T(4,128)(2,1)S(1)}, u32[]{:S(2)}, u32[]{:S(2)}) async-start(bf16[64,3,1024]{2,1,0:T(4,128)(2,1)} %all_to_all.24), calls=%async_computation.2 | async-start | bytes 1048576 | tf_op jit(solution)/shard_map/all_to_all | solution.py:173
Sparse Core Ops, SparseCore 0:
  16.9 44.1 all-gather.2
